TPU v7x, 32 devices: a whole 2x2x4 slice. The times are simulated.
32 devices in a mesh: col: 32 (over z, y, x, core).
Axes of the slice: x: 2, y: 2, z: 4, core: 2. Of those that a mesh axis runs over, the one named last changes fastest.
Arguments:
- covariance: float32 [2, 8192, 8192], P(None, 'col'), may hold values from -6 to 6, as said below
- forcing: float32 [2, 8192, 8192], P(None, 'col'), may hold values from -24 to 24, as said below
- coefficient: float32 [2, 64, 128], replicated, may hold values from 0.5 to 1.5
- y_operator: float32 [2, 64, 64], replicated, may hold values from -0.75 to 0.75
- z_operator: float32 [2, 128, 128], replicated, may hold values from -0.5 to 0.5
Outputs:
- advanced: float32 [2, 8192, 8192], P(None, 'col')
Inputs may be any that keep to these rules, and one draw needn't show every extreme that they name: Each harmonic's covariance is symmetric. Each harmonic's forcing is symmetric.
All inputs are finite; a program needn't handle non-finite values.
Results may differ from a plain program's by a relative error of at most 0.0001.
Values sent between devices are 32-bit elements; how exact they have to be, the bound alone decides.
No kernel may reach another device: no remote copies, remote signals or barrier semaphores. Data moves between devices by JAX's collectives and lax.ppermute only.
A program may use at most 256 MiB of HBM per device.

v0:
```python
import jax
import jax.numpy as jnp
from jax import lax
from jax.sharding import PartitionSpec as P

step_size = 0.2


def combined(values, y_operator, z_operator):
    along_y = jnp.einsum("hya,hacz->hycz", y_operator, values, precision=lax.Precision.HIGHEST)
    along_z = jnp.einsum("hycb,hzb->hycz", values, z_operator, precision=lax.Precision.HIGHEST)
    return along_y + along_z


def apply_operator(row_slab, y_operator, z_operator, coefficient):
    grid_y = y_operator.shape[1]
    grid_z = z_operator.shape[1]
    width = row_slab.shape[1]
    grid = jnp.swapaxes(row_slab.reshape(2, width, grid_y, grid_z), 1, 2)
    inner = coefficient[:, :, None, :] * combined(grid, y_operator, z_operator)
    outer = combined(inner, y_operator, z_operator)
    return jnp.swapaxes(outer, 1, 2).reshape(row_slab.shape)


def transpose_slab(product):
    width = product.shape[1]
    groups = lax.axis_size("col")
    received = lax.all_to_all(product, "col", split_axis=2, concat_axis=2, tiled=True)
    blocks = received.reshape(2, width, groups, width)
    return jnp.swapaxes(blocks, 1, 3).reshape(2, width, groups * width)


def on_device(covariance, forcing, coefficient, y_operator, z_operator):

    def slope_of(state):
        product = apply_operator(state, y_operator, z_operator, coefficient)
        return product + transpose_slab(product) + forcing

    slope_one = slope_of(covariance)
    slope_two = slope_of(covariance + 0.5 * step_size * slope_one)
    slope_three = slope_of(covariance + 0.5 * step_size * slope_two)
    slope_four = slope_of(covariance + step_size * slope_three)
    return covariance + step_size / 6.0 * (
        slope_one + 2.0 * slope_two + 2.0 * slope_three + slope_four
    )


def solution(mesh):
    placed = (P(None, "col", None), P(None, "col", None), P(), P(), P())
    return jax.shard_map(
        on_device, mesh=mesh, in_specs=placed, out_specs=P(None, "col", None), check_vma=False
    )
```

profile of v0, /device:TPU:0, one launch (start us, length us, event | category | flops | bytes accessed | tf_op | source)
XLA Modules:
  0.0 2336.2 jit_solution(9964949854036722242)
XLA Ops:
  35.9 22.5 add_multiply_fusion
  80.2 22.6 bitcast_add_fusion.6
  121.1 24.9 %copy.35 = f32[2,256,8192]{1,0,2:T(2,128)} copy(f32[2,256,8192]{2,1,0:T(8,128)} %reshape.50) | data formatting | bytes 33554432 | tf_op jit(solution)/shard_map/reshape | solution.py:22
  146.0 370.6 %all_to_all.20 = f32[2,256,8192]{1,0,2:T(2,128)S(1)} all-to-all(f32[2,256,8192]{1,0,2:T(2,128)} %copy.35), channel_id=1, replica_groups=mesh['col'=32] {'col'}, dimensions={2} | all-to-all | bytes 33554432 | tf_op jit(solution)/shard_map/all_to_all | solution.py:28
  551.2 28.2 %multiply_add_fusion.3 = f32[2,256,8192]{2,1,0:T(8,128)} fusion(f32[2,256,8192]{2,1,0:T(8,128)} %param.5, f32[2,256,8192]{2,1,0:T(8,128)} %param.6, f32[2,256,8192]{2,1,0:T(8,128)} %reshape.50, f32[2,256,8192]{2,1,0:T(8,128)} %reshape.52), kind=kLoop, calls=%fused_computation.27 | loop fusion | flops 16777216 | bytes 83886080 | tf_op jit(solution)/shard_map/add | solution.py:40
  593.4 22.1 fusion.4
  615.5 22.2 fusion.10
  659.7 22.3 bitcast_add_fusion.4
  700.1 25.0 %copy.42 = f32[2,256,8192]{1,0,2:T(2,128)} copy(f32[2,256,8192]{2,1,0:T(8,128)} %reshape.54) | data formatting | bytes 33554432 | tf_op jit(solution)/shard_map/reshape | solution.py:22
  725.1 367.5 %all_to_all.21 = f32[2,256,8192]{1,0,2:T(2,128)S(1)} all-to-all(f32[2,256,8192]{1,0,2:T(2,128)} %copy.42), channel_id=1, replica_groups=mesh['col'=32] {'col'}, dimensions={2} | all-to-all | bytes 33554432 | tf_op jit(solution)/shard_map/all_to_all | solution.py:28
  1127.1 28.2 %multiply_add_fusion.2 = f32[2,256,8192]{2,1,0:T(8,128)} fusion(f32[2,256,8192]{2,1,0:T(8,128)} %param.5, f32[2,256,8192]{2,1,0:T(8,128)} %param.6, f32[2,256,8192]{2,1,0:T(8,128)} %reshape.54, f32[2,256,8192]{2,1,0:T(8,128)} %reshape.56), kind=kLoop, calls=%fused_computation.25 | loop fusion | flops 16777216 | bytes 83886080 | tf_op jit(solution)/shard_map/add | solution.py:41
  1169.3 22.0 fusion.2
  1191.3 22.3 fusion.9
  1213.6 22.0 fusion.22
  1235.6 22.3 bitcast_add_fusion.2
  1276.0 25.0 %copy.49 = f32[2,256,8192]{1,0,2:T(2,128)} copy(f32[2,256,8192]{2,1,0:T(8,128)} %reshape.58) | data formatting | bytes 33554432 | tf_op jit(solution)/shard_map/reshape | solution.py:22
  1301.0 367.6 %all_to_all.22 = f32[2,256,8192]{1,0,2:T(2,128)S(1)} all-to-all(f32[2,256,8192]{1,0,2:T(2,128)} %copy.49), channel_id=1, replica_groups=mesh['col'=32] {'col'}, dimensions={2} | all-to-all | bytes 33554432 | tf_op jit(solution)/shard_map/all_to_all | solution.py:28
  1703.1 28.1 %multiply_add_fusion.1 = f32[2,256,8192]{2,1,0:T(8,128)} fusion(f32[2,256,8192]{2,1,0:T(8,128)} %param.5, f32[2,256,8192]{2,1,0:T(8,128)} %param.6, f32[2,256,8192]{2,1,0:T(8,128)} %reshape.58, f32[2,256,8192]{2,1,0:T(8,128)} %reshape.60), kind=kLoop, calls=%fused_computation.23 | loop fusion | flops 16777216 | bytes 83886080 | tf_op jit(solution)/shard_map/add | solution.py:42
  1767.2 22.3 fusion.8
  1789.4 21.9 fusion.19
  1811.4 22.3 bitcast_add_fusion
  1851.8 25.0 %copy.56 = f32[2,256,8192]{1,0,2:T(2,128)} copy(f32[2,256,8192]{2,1,0:T(8,128)} %reshape.62) | data formatting | bytes 33554432 | tf_op jit(solution)/shard_map/reshape | solution.py:22
  1876.8 367.4 %all_to_all.23 = f32[2,256,8192]{1,0,2:T(2,128)S(1)} all-to-all(f32[2,256,8192]{1,0,2:T(2,128)} %copy.56), channel_id=1, replica_groups=mesh['col'=32] {'col'}, dimensions={2} | all-to-all | bytes 33554432 | tf_op jit(solution)/shard_map/all_to_all | solution.py:28
  2278.6 57.2 %multiply_add_fusion = f32[2,256,8192]{2,1,0:T(8,128)} fusion(f32[2,256,8192]{2,1,0:T(8,128)} %param.5, f32[2,256,8192]{2,1,0:T(8,128)} %param.6, f32[2,256,8192]{2,1,0:T(8,128)} %reshape.62, f32[2,256,8192]{2,1,0:T(8,128)} %reshape.64, f32[2,256,8192]{2,1,0:T(8,128)} %reshape.50, f32[2,256,8192]{2,1,0:T(8,128)} %reshape.52, f32[2,256,8192]{2,1,0:T(8,128)} %reshape.54, ...), kind=kLoop, calls=%fused_computation.22 | loop fusion | flops 62914560 | bytes 184549376 | tf_op jit(solution)/shard_map/add | solution.py:43
  (26 shorter events, 354.5 us)
Async XLA Ops:
  0.0 35.9 %copy-start = (f32[2,128,128]{2,1,0:T(8,128)S(1)}, f32[2,128,128]{2,1,0:T(8,128)}, u32[]{:S(2)}) copy-start(f32[2,128,128]{2,1,0:T(8,128)} %param.9) | copy-start | bytes 393220
  0.0 14.2 copy-start.2
  14.2 21.6 copy-start.1
where the time goes:
time: 2350 us; the launch traced here: 2340 us
  blocking collectives  1470 us (63%)
  local copies, waits for them, and re-layouts  367 us (16%)
  matrix products  354 us (15%)
  other arithmetic  142 us (6%)
    all_to_all x4, blocking collectives, transpose_slab(): lax.all_to_all(product, 'col', split_axis=2, concat_axis=2, tiled=True)  1470 us
    dot_general x8, matrix products, combined(): jnp.einsum('hycb,hzb->hycz', values, z_operator, precision=lax.Precision....  179 us
    dot_general x8, matrix products, combined(): jnp.einsum('hya,hacz->hycz', y_operator, values, precision=lax.Precision....  175 us
    reshape x8, local copies, waits for them, and re-layouts, apply_operator(): return jnp.swapaxes(outer, 1, 2).reshape(row_slab.shape)  173 us
    reshape x4, local copies, waits for them, and re-layouts, transpose_slab(): return jnp.swapaxes(blocks, 1, 3).reshape(2, width, groups * width)  72.8 us
    transpose x4, local copies, waits for them, and re-layouts, transpose_slab(): return jnp.swapaxes(blocks, 1, 3).reshape(2, width, groups * width)  65 us
    add x1, other arithmetic, on_device(): covariance + step_size / 6.0 * (slope_one + 2.0 * slope_two + 2.0 * slope...  57.2 us
    unnamed x10, local copies, waits for them, and re-layouts  56.5 us

commit v1 on v0

v1 whole, which is shorter than its diff:
```python
import functools

import jax
import jax.numpy as jnp
from jax import lax
from jax.experimental import pallas as pl
from jax.experimental.pallas import tpu as pltpu
from jax.sharding import PartitionSpec as P

step_size = 0.2
lanes = 128
sublanes = 8
tiles = 4
group = 8


def split(value):
    high = value.astype(jnp.bfloat16)
    low = (value - high.astype(jnp.float32)).astype(jnp.bfloat16)
    return high, low


def operator_pair(value):
    high = lax.reduce_precision(value, exponent_bits=8, mantissa_bits=7)
    return high.astype(jnp.bfloat16), (value - high).astype(jnp.bfloat16)


def combined(rows, y_pair, z_pair):
    grid_y = rows[0].shape[0]
    pairs = [split(row) for row in rows]
    right = jnp.concatenate([jnp.concatenate(pair, axis=0) for pair in pairs], axis=1)
    left = jnp.concatenate([jnp.concatenate(pair, axis=1) for pair in pairs], axis=0)
    along_y = jnp.dot(y_pair, right, preferred_element_type=jnp.float32)
    along_z = jnp.dot(left, z_pair, preferred_element_type=jnp.float32)
    out = []
    for i in range(len(rows)):
        y_part = along_y[:, i * lanes : (i + 1) * lanes]
        z_part = along_z[i * grid_y : (i + 1) * grid_y]
        out.append(
            (y_part[:grid_y] + y_part[grid_y:]) + (z_part[:, :lanes] + z_part[:, lanes:])
        )
    return out


def operate(rows, y_pair, z_pair, gain):
    inner = [gain * row for row in combined(rows, y_pair, z_pair)]
    return combined(inner, y_pair, z_pair)


def body(stage, grid_y, *refs):
    y_ref, z_ref, gain_ref, *ins = refs[: 3 + {"first": 1, "second": 3, "third": 4}[stage]]
    outs = refs[3 + len(ins) :]
    result_ref, sent_ref = outs[0], outs[1]
    inner = pl.program_id(1)
    y_pair, z_pair, gain = y_ref[0], z_ref[0], gain_ref[0]

    def tiled(ref, t, r):
        return ref[0, t, pl.ds(r, grid_y, stride=sublanes), :]

    def arrived(ref, t, r):
        flat = ref.reshape(grid_y * tiles * sublanes, lanes)
        return flat[pl.ds(t * sublanes + r, grid_y, stride=tiles * sublanes), :]

    def per_tile(t, carry):
        for r0 in range(0, sublanes, group):
            each = range(r0, r0 + group)
            if stage == "first":
                (state,) = ins
                out = operate([tiled(state, t, r) for r in each], y_pair, z_pair, gain)
            elif stage == "second":
                product, crossed, forcing = ins
                slopes = [
                    tiled(product, t, r) + arrived(crossed, t, r) + step_size * tiled(forcing, t, r)
                    for r in each
                ]
                for r, slope in zip(each, slopes):
                    outs[2][0, t, r] = slope
                out = operate(slopes, y_pair, z_pair, gain)
            else:
                product, crossed, slope, state = ins
                firsts = [
                    slope[0, t, r] * (1 / 6)
                    + arrived(crossed, t, r) * 0.125
                    + tiled(product, t, r) * (1 / 24)
                    for r in each
                ]
                seconds = [
                    slope[0, t, r] * 0.5 + arrived(crossed, t, r) * (1 / 6) + value
                    for r, value in zip(each, operate(firsts, y_pair, z_pair, gain))
                ]
                out = [
                    0.5 * (slope[0, t, r] + tiled(state, t, r)) + value
                    for r, value in zip(each, operate(seconds, y_pair, z_pair, gain))
                ]
            for r, value in zip(each, out):
                result_ref[0, inner * tiles + t, pl.ds(r, grid_y, stride=sublanes), :] = value
        return carry

    lax.fori_loop(0, tiles, per_tile, 0)

    @pl.when(inner == pl.num_programs(1) - 1)
    def _():
        owners, _, columns = sent_ref.shape[:3]

        def per_owner(d, carry):
            for c in range(columns):
                start = pl.multiple_of((d * columns + c) * sublanes, sublanes)
                block = result_ref[0, :, pl.ds(start, sublanes), :].reshape(lanes, lanes)
                sent_ref[d, 0, c] = block.T
            return carry

        lax.fori_loop(0, owners, per_owner, 0)


def stage_call(stage, harmonic, groups, grid_y, width, y_pair, z_pair, gain, *operands):
    chunk = tiles * sublanes
    inner = lanes // chunk
    per = width // lanes
    row_tiles = width // sublanes
    rows = grid_y * sublanes

    def whole(shape):
        return pl.BlockSpec((1, *shape), lambda k, i: (harmonic, 0, 0))

    def tile_spec(which):
        return pl.BlockSpec((1, tiles, rows, lanes), lambda k, i: (which, k * inner + i, 0, 0))

    crossed = pl.BlockSpec((grid_y, chunk, lanes), lambda k, i: (0, k * inner + i, 0))
    slope = pl.BlockSpec(
        (1, tiles, sublanes, grid_y, lanes), lambda k, i: (0, k * inner + i, 0, 0, 0)
    )
    ins = {
        "first": [tile_spec(harmonic)],
        "second": [tile_spec(0), crossed, tile_spec(harmonic)],
        "third": [tile_spec(0), crossed, slope, tile_spec(harmonic)],
    }[stage]
    out_specs = [
        pl.BlockSpec((1, lanes // sublanes, rows, lanes), lambda k, i: (0, k, 0, 0)),
        pl.BlockSpec((groups, 1, per, lanes, lanes), lambda k, i: (0, k, 0, 0, 0)),
    ]
    out_shape = [
        jax.ShapeDtypeStruct((1, row_tiles, rows, lanes), jnp.float32),
        jax.ShapeDtypeStruct((groups, per, per, lanes, lanes), jnp.float32),
    ]
    if stage == "second":
        out_specs.append(slope)
        out_shape.append(
            jax.ShapeDtypeStruct((1, row_tiles, sublanes, grid_y, lanes), jnp.float32)
        )
    passes = 2 if stage == "third" else 1
    return pl.pallas_call(
        functools.partial(body, stage, grid_y),
        grid=(per, inner),
        in_specs=[
            whole((2 * grid_y, 2 * grid_y)),
            whole((2 * lanes, 2 * lanes)),
            whole((grid_y, lanes)),
            *ins,
        ],
        out_specs=out_specs,
        out_shape=out_shape,
        cost_estimate=pl.CostEstimate(
            flops=passes * 16 * width * grid_y * lanes * (grid_y + lanes),
            bytes_accessed=(len(ins) + len(out_specs)) * width * grid_y * lanes * 4,
            transcendentals=0,
        ),
        compiler_params=pltpu.CompilerParams(vmem_limit_bytes=60 * 1024 * 1024),
        name=f"{stage}_{harmonic}",
    )(y_pair, z_pair, gain, *operands)


def finish_body(per_step, *refs):
    product_ref, crossed_ref, out_ref = refs[0], refs[1], refs[-1]
    for j in range(per_step):
        half = product_ref[0, :, j * sublanes : (j + 1) * sublanes, :]
        out_ref[0, :, j * lanes : (j + 1) * lanes] = half.reshape(-1, lanes) + crossed_ref[j]


def finish_call(harmonic, product, crossed, out):
    grid_y, width, _ = crossed.shape
    per_step = 8 if grid_y % 8 == 0 else 1
    row_tiles = width // sublanes
    in_specs = [
        pl.BlockSpec((1, row_tiles, per_step * sublanes, lanes), lambda i: (0, 0, i, 0)),
        pl.BlockSpec((per_step, width, lanes), lambda i: (i, 0, 0)),
    ]
    operands = [product, crossed]
    aliases = {}
    if out is not None:
        in_specs.append(pl.BlockSpec(memory_space=pl.ANY))
        operands.append(out)
        aliases = {2: 0}
    return pl.pallas_call(
        functools.partial(finish_body, per_step),
        grid=(grid_y // per_step,),
        in_specs=in_specs,
        out_specs=pl.BlockSpec((1, width, per_step * lanes), lambda i: (harmonic, 0, i)),
        out_shape=jax.ShapeDtypeStruct((2, width, grid_y * lanes), jnp.float32),
        input_output_aliases=aliases,
        cost_estimate=pl.CostEstimate(
            flops=width * grid_y * lanes,
            bytes_accessed=3 * width * grid_y * lanes * 4,
            transcendentals=0,
        ),
        compiler_params=pltpu.CompilerParams(vmem_limit_bytes=48 * 1024 * 1024),
        name=f"finish_{harmonic}",
    )(*operands)


def exchange(sent):
    received = lax.all_to_all(sent, "col", split_axis=0, concat_axis=0, tiled=True)
    groups, per = sent.shape[:2]
    return received.reshape(groups * per, per * lanes, lanes)


def on_device_tiled(covariance, forcing, coefficient, y_operator, z_operator):
    groups = lax.axis_size("col")
    width = covariance.shape[1]
    grid_y = y_operator.shape[1]

    def by_tiles(value):
        cut = value.reshape(2, width // sublanes, sublanes, grid_y, lanes)
        return jnp.swapaxes(cut, 2, 3).reshape(2, width // sublanes, grid_y * sublanes, lanes)

    y_high, y_low = operator_pair(y_operator)
    z_high, z_low = operator_pair(jnp.swapaxes(z_operator, 1, 2))
    y_pair = jnp.concatenate(
        [jnp.concatenate([y_high, y_high], axis=2), jnp.concatenate([y_low, y_low], axis=2)], axis=1
    )
    z_pair = jnp.concatenate([jnp.concatenate([z_high, z_low], axis=2)] * 2, axis=1)
    gain = step_size * coefficient
    state, source = by_tiles(covariance), by_tiles(forcing)

    def call(stage, harmonic, *operands):
        return stage_call(
            stage, harmonic, groups, grid_y, width, y_pair, z_pair, gain, *operands
        )

    first = [call("first", h, state) for h in range(2)]
    crossed = [exchange(sent) for _, sent in first]
    second = [call("second", h, first[h][0], crossed[h], source) for h in range(2)]
    crossed = [exchange(sent) for _, sent, _ in second]
    third = [call("third", h, second[h][0], crossed[h], second[h][2], state) for h in range(2)]
    crossed = [exchange(sent) for _, sent in third]
    out = None
    for h in range(2):
        out = finish_call(h, third[h][0], crossed[h], out)
    return out


def on_device_plain(covariance, forcing, coefficient, y_operator, z_operator):
    grid_y, grid_z = y_operator.shape[1], z_operator.shape[1]
    width = covariance.shape[1]
    groups = lax.axis_size("col")

    def along(values):
        part = jnp.einsum("hya,hcaz->hcyz", y_operator, values, precision=lax.Precision.HIGHEST)
        other = jnp.einsum("hcyb,hzb->hcyz", values, z_operator, precision=lax.Precision.HIGHEST)
        return part + other

    def operated(slab):
        grid = slab.reshape(2, width, grid_y, grid_z)
        return along(step_size * coefficient[:, None] * along(grid)).reshape(slab.shape)

    def crossed(product):
        received = lax.all_to_all(product, "col", split_axis=2, concat_axis=2, tiled=True)
        blocks = received.reshape(2, width, groups, width)
        return jnp.swapaxes(blocks, 1, 3).reshape(2, width, groups * width)

    product = operated(covariance)
    slope = product + crossed(product) + step_size * forcing
    product = operated(slope)
    other = crossed(product)
    inner = slope / 2 + other / 6 + operated(slope / 6 + other / 8 + product / 24)
    half = (covariance + slope) / 2 + operated(inner)
    return half + crossed(half)


def on_device(covariance, forcing, coefficient, y_operator, z_operator):
    width = covariance.shape[1]
    grid_y, grid_z = y_operator.shape[1], z_operator.shape[1]
    tiled = grid_z == lanes and width % lanes == 0 and grid_y % 16 == 0
    chosen = on_device_tiled if tiled else on_device_plain
    return chosen(covariance, forcing, coefficient, y_operator, z_operator)


def solution(mesh):
    placed = (P(None, "col", None), P(None, "col", None), P(), P(), P())
    return jax.shard_map(
        on_device, mesh=mesh, in_specs=placed, out_specs=P(None, "col", None), check_vma=False
    )
```

time: 2350 us -> 1190 us (0.51)
  blocking collectives: 1470 us -> 0 us
  waiting for transfers between devices: 0 us -> 904 us
  local copies, waits for them, and re-layouts: 367 us -> 1 us
  matrix products: 354 us -> 0 us
  Pallas kernels: 0 us -> 253 us
  other arithmetic: 142 us -> 3.78 us
  starting transfers between devices: 0 us -> 25.9 us
    all_to_all x4 -> x0, blocking collectives: 1470 us -> none  [transpose_slab(): lax.all_to_all(product, 'col', split_axis=2, concat_axis=2, tiled=True)]
    all_to_all x0 -> x6, waiting for transfers between devices: none -> 904 us  [exchange(): lax.all_to_all(sent, 'col', split_axis=0, concat_axis=0, tiled=True)]
    dot_general x16 -> x0, matrix products: 354 us -> none  [the longest x8 179 us: combined(): jnp.einsum('hycb,hzb->hycz', values, z_operator, precision=lax.Precision....]
    pallas_call x0 -> x8, Pallas kernels: none -> 253 us  [the longest x6 231 us: stage_call(): pl.pallas_call(functools.partial(body, stage, grid_y), grid=(per, inner),...]
    reshape x12 -> x0, local copies, waits for them, and re-layouts: 246 us -> none  [the longest x8 173 us: apply_operator(): return jnp.swapaxes(outer, 1, 2).reshape(row_slab.shape)]
    add x4 -> x0, other arithmetic: 142 us -> none  [the longest x1 57.2 us: on_device(): covariance + step_size / 6.0 * (slope_one + 2.0 * slope_two + 2.0 * slope...]
    transpose x4 -> x0, local copies, waits for them, and re-layouts: 65 us -> none  [transpose_slab(): return jnp.swapaxes(blocks, 1, 3).reshape(2, width, groups * width)]
    unnamed x10 -> x1, local copies, waits for them, and re-layouts: 56.5 us -> 1 us
  transfers between devices with their start and end apart: 0 -> 6, of which waited for: 0 -> 6; matrix products, arithmetic and copies ran while one was open for 0% -> 0% of each run, Pallas kernels for 0% -> 18%
where the time goes in v1:
time: 1190 us
  waiting for transfers between devices  904 us (76%)
  Pallas kernels  253 us (21%)
  starting transfers between devices  25.9 us (2%)
    all_to_all x6, waiting for transfers between devices, exchange(): lax.all_to_all(sent, 'col', split_axis=0, concat_axis=0, tiled=True)  904 us
    pallas_call x6, Pallas kernels, stage_call(): pl.pallas_call(functools.partial(body, stage, grid_y), grid=(per, inner),...  231 us
    all_to_all x6, starting transfers between devices, exchange(): lax.all_to_all(sent, 'col', split_axis=0, concat_axis=0, tiled=True)  25.9 us
  transfers between devices with their start and end apart: 6, of which 6 were waited for; matrix products, arithmetic and copies ran while one was open for 0% of the time, Pallas kernels for 18%

profile of v1, /device:TPU:0, one launch (start us, length us, event | category | flops | bytes accessed | tf_op | source)
XLA Modules:
  0.0 1187.7 jit_solution(12615747123790633221)
XLA Ops:
  0.0 1.5 broadcast_multiply_fusion.refs_2_
  1.5 0.9 reduce-precision_convert_fusion.1
  2.3 1.0 copy.7
  4.1 0.7 maximum_maximum_fusion.refs_1_
  4.8 29.9 %first_0.1 = (f32[1,32,512,128]{3,2,1,0:T(8,128)}, f32[32,2,2,128,128]{4,3,2,1,0:T(8,128)}) custom-call(bf16[2,128,128]{2,1,0:T(8,128)(2,1)} %maximum_maximum_fusion.1.refs_0_, bf16[2,256,256]{2,1,0:T(8,128)(2,1)} %maximum_maximum_fusion.refs_1_, f32[2,64,128]{2,1,0:T(8,128)} %broadcast_multiply_fusion.refs_2_, f32[2,32,512,128]{3,2,1,0:T(8,128)} %bitcast.21), custom_call_target="tpu_custom_call" | custom-call | flops 6442450944 | bytes 25165824 | tf_op jit(solution)/shard_map/first_0/pallas_call | solution.py:151
  34.7 7.5 all-to-all-start.3
  42.1 30.0 %first_1.1 = (f32[1,32,512,128]{3,2,1,0:T(8,128)}, f32[32,2,2,128,128]{4,3,2,1,0:T(8,128)}) custom-call(bf16[2,128,128]{2,1,0:T(8,128)(2,1)} %maximum_maximum_fusion.1.refs_0_, bf16[2,256,256]{2,1,0:T(8,128)(2,1)} %maximum_maximum_fusion.refs_1_, f32[2,64,128]{2,1,0:T(8,128)} %broadcast_multiply_fusion.refs_2_, f32[2,32,512,128]{3,2,1,0:T(8,128)} %bitcast.22), custom_call_target="tpu_custom_call" | custom-call | flops 6442450944 | bytes 25165824 | tf_op jit(solution)/shard_map/first_1/pallas_call | solution.py:151
  72.2 155.9 %all-to-all-done.3 = f32[32,2,2,128,128]{4,3,2,1,0:T(8,128)} async-done(((f32[32,2,2,128,128]{4,3,2,1,0:T(8,128)}), f32[32,2,2,128,128]{4,3,2,1,0:T(8,128)}, u32[]{:S(2)}, u32[]{:S(2)}) %all-to-all-start.3) | async-done | bytes 8388640 | tf_op jit(solution)/shard_map/all_to_all | solution.py:211
  228.0 3.7 all-to-all-start
  231.7 38.4 %second_0.1 = (f32[1,32,512,128]{3,2,1,0:T(8,128)}, f32[32,2,2,128,128]{4,3,2,1,0:T(8,128)}, f32[1,32,8,64,128]{4,3,2,1,0:T(8,128)}) custom-call(bf16[2,128,128]{2,1,0:T(8,128)(2,1)} %maximum_maximum_fusion.1.refs_0_, bf16[2,256,256]{2,1,0:T(8,128)(2,1)} %maximum_maximum_fusion.refs_1_, f32[2,64,128]{2,1,0:T(8,128)} %broadcast_multiply_fusion.refs_2_, ...), custom_call_target="tpu_custom_call" | custom-call | flops 6442450944 | bytes 50331648 | tf_op jit(solution)/shard_map/second_0/pallas_call | solution.py:151
  270.2 147.6 %all-to-all-done = f32[32,2,2,128,128]{4,3,2,1,0:T(8,128)} async-done(((f32[32,2,2,128,128]{4,3,2,1,0:T(8,128)}), f32[32,2,2,128,128]{4,3,2,1,0:T(8,128)}, u32[]{:S(2)}, u32[]{:S(2)}) %all-to-all-start) | async-done | bytes 8388640 | tf_op jit(solution)/shard_map/all_to_all | solution.py:211
  417.8 3.7 all-to-all-start.4
  421.4 38.3 %second_1.1 = (f32[1,32,512,128]{3,2,1,0:T(8,128)}, f32[32,2,2,128,128]{4,3,2,1,0:T(8,128)}, f32[1,32,8,64,128]{4,3,2,1,0:T(8,128)}) custom-call(bf16[2,128,128]{2,1,0:T(8,128)(2,1)} %maximum_maximum_fusion.1.refs_0_, bf16[2,256,256]{2,1,0:T(8,128)(2,1)} %maximum_maximum_fusion.refs_1_, f32[2,64,128]{2,1,0:T(8,128)} %broadcast_multiply_fusion.refs_2_, ...), custom_call_target="tpu_custom_call" | custom-call | flops 6442450944 | bytes 50331648 | tf_op jit(solution)/shard_map/second_1/pallas_call | solution.py:151
  459.8 147.7 %all-to-all-done.4 = f32[32,2,2,128,128]{4,3,2,1,0:T(8,128)} async-done(((f32[32,2,2,128,128]{4,3,2,1,0:T(8,128)}), f32[32,2,2,128,128]{4,3,2,1,0:T(8,128)}, u32[]{:S(2)}, u32[]{:S(2)}) %all-to-all-start.4) | async-done | bytes 8388640 | tf_op jit(solution)/shard_map/all_to_all | solution.py:211
  607.5 3.7 all-to-all-start.1
  611.2 47.4 %third_0.1 = (f32[1,32,512,128]{3,2,1,0:T(8,128)}, f32[32,2,2,128,128]{4,3,2,1,0:T(8,128)}) custom-call(bf16[2,128,128]{2,1,0:T(8,128)(2,1)} %maximum_maximum_fusion.1.refs_0_, bf16[2,256,256]{2,1,0:T(8,128)(2,1)} %maximum_maximum_fusion.refs_1_, f32[2,64,128]{2,1,0:T(8,128)} %broadcast_multiply_fusion.refs_2_, ...), custom_call_target="tpu_custom_call" | custom-call | flops 12884901888 | bytes 50331648 | tf_op jit(solution)/shard_map/third_0/pallas_call | solution.py:151
  658.6 138.7 %all-to-all-done.1 = f32[32,2,2,128,128]{4,3,2,1,0:T(8,128)} async-done(((f32[32,2,2,128,128]{4,3,2,1,0:T(8,128)}), f32[32,2,2,128,128]{4,3,2,1,0:T(8,128)}, u32[]{:S(2)}, u32[]{:S(2)}) %all-to-all-start.1) | async-done | bytes 8388640 | tf_op jit(solution)/shard_map/all_to_all | solution.py:211
  797.2 3.7 all-to-all-start.5
  800.9 47.1 %third_1.1 = (f32[1,32,512,128]{3,2,1,0:T(8,128)}, f32[32,2,2,128,128]{4,3,2,1,0:T(8,128)}) custom-call(bf16[2,128,128]{2,1,0:T(8,128)(2,1)} %maximum_maximum_fusion.1.refs_0_, bf16[2,256,256]{2,1,0:T(8,128)(2,1)} %maximum_maximum_fusion.refs_1_, f32[2,64,128]{2,1,0:T(8,128)} %broadcast_multiply_fusion.refs_2_, ...), custom_call_target="tpu_custom_call" | custom-call | flops 12884901888 | bytes 50331648 | tf_op jit(solution)/shard_map/third_1/pallas_call | solution.py:151
  848.1 138.9 %all-to-all-done.5 = f32[32,2,2,128,128]{4,3,2,1,0:T(8,128)} async-done(((f32[32,2,2,128,128]{4,3,2,1,0:T(8,128)}), f32[32,2,2,128,128]{4,3,2,1,0:T(8,128)}, u32[]{:S(2)}, u32[]{:S(2)}) %all-to-all-start.5) | async-done | bytes 8388640 | tf_op jit(solution)/shard_map/all_to_all | solution.py:211
  986.9 3.7 all-to-all-start.2
  990.6 11.0 finish_0.1.refs_2_
  1001.7 175.0 %all-to-all-done.2 = f32[32,2,2,128,128]{4,3,2,1,0:T(8,128)} async-done(((f32[32,2,2,128,128]{4,3,2,1,0:T(8,128)}), f32[32,2,2,128,128]{4,3,2,1,0:T(8,128)}, u32[]{:S(2)}, u32[]{:S(2)}) %all-to-all-start.2) | async-done | bytes 8388640 | tf_op jit(solution)/shard_map/all_to_all | solution.py:211
  1176.7 11.0 finish_1.1
  (2 shorter events, 0.7 us)
Async XLA Ops:
  34.7 193.4 %all-to-all-start.3 = ((f32[32,2,2,128,128]{4,3,2,1,0:T(8,128)}), f32[32,2,2,128,128]{4,3,2,1,0:T(8,128)}, u32[]{:S(2)}, u32[]{:S(2)}) async-start(f32[32,2,2,128,128]{4,3,2,1,0:T(8,128)} %get-tuple-element.27), calls=%async_computation.3 | async-start | bytes 16777216 | tf_op jit(solution)/shard_map/all_to_all | solution.py:211
  228.0 189.7 %all-to-all-start = ((f32[32,2,2,128,128]{4,3,2,1,0:T(8,128)}), f32[32,2,2,128,128]{4,3,2,1,0:T(8,128)}, u32[]{:S(2)}, u32[]{:S(2)}) async-start(f32[32,2,2,128,128]{4,3,2,1,0:T(8,128)} %get-tuple-element.20), calls=%async_computation | async-start | bytes 16777216 | tf_op jit(solution)/shard_map/all_to_all | solution.py:211
  417.8 189.7 %all-to-all-start.4 = ((f32[32,2,2,128,128]{4,3,2,1,0:T(8,128)}), f32[32,2,2,128,128]{4,3,2,1,0:T(8,128)}, u32[]{:S(2)}, u32[]{:S(2)}) async-start(f32[32,2,2,128,128]{4,3,2,1,0:T(8,128)} %get-tuple-element.29), calls=%async_computation.4 | async-start | bytes 16777216 | tf_op jit(solution)/shard_map/all_to_all | solution.py:211
  607.5 189.7 %all-to-all-start.1 = ((f32[32,2,2,128,128]{4,3,2,1,0:T(8,128)}), f32[32,2,2,128,128]{4,3,2,1,0:T(8,128)}, u32[]{:S(2)}, u32[]{:S(2)}) async-start(f32[32,2,2,128,128]{4,3,2,1,0:T(8,128)} %get-tuple-element.22), calls=%async_computation.1 | async-start | bytes 16777216 | tf_op jit(solution)/shard_map/all_to_all | solution.py:211
  797.2 189.7 %all-to-all-start.5 = ((f32[32,2,2,128,128]{4,3,2,1,0:T(8,128)}), f32[32,2,2,128,128]{4,3,2,1,0:T(8,128)}, u32[]{:S(2)}, u32[]{:S(2)}) async-start(f32[32,2,2,128,128]{4,3,2,1,0:T(8,128)} %get-tuple-element.32), calls=%async_computation.5 | async-start | bytes 16777216 | tf_op jit(solution)/shard_map/all_to_all | solution.py:211
  986.9 189.7 %all-to-all-start.2 = ((f32[32,2,2,128,128]{4,3,2,1,0:T(8,128)}), f32[32,2,2,128,128]{4,3,2,1,0:T(8,128)}, u32[]{:S(2)}, u32[]{:S(2)}) async-start(f32[32,2,2,128,128]{4,3,2,1,0:T(8,128)} %get-tuple-element.25), calls=%async_computation.2 | async-start | bytes 16777216 | tf_op jit(solution)/shard_map/all_to_all | solution.py:211

commit v2 on v1

--- a/solution.py
+++ b/solution.py
@@ -18,11 +18,6 @@
     high = value.astype(jnp.bfloat16)
     low = (value - high.astype(jnp.float32)).astype(jnp.bfloat16)
     return high, low
-
-
-def operator_pair(value):
-    high = lax.reduce_precision(value, exponent_bits=8, mantissa_bits=7)
-    return high.astype(jnp.bfloat16), (value - high).astype(jnp.bfloat16)
 
 
 def combined(rows, y_pair, z_pair):
@@ -47,45 +42,79 @@
     return combined(inner, y_pair, z_pair)
 
 
+def prepare(y_ref, z_ref, y_pair_ref, z_pair_ref):
+    grid_y = y_ref.shape[1]
+    for part, value in enumerate(split(y_ref[0])):
+        for side in range(2):
+            y_pair_ref[pl.ds(part * grid_y, grid_y), pl.ds(side * grid_y, grid_y)] = value
+    for part, value in enumerate(split(z_ref[0].T)):
+        for side in range(2):
+            z_pair_ref[pl.ds(side * lanes, lanes), pl.ds(part * lanes, lanes)] = value
+
+
 def body(stage, grid_y, *refs):
-    y_ref, z_ref, gain_ref, *ins = refs[: 3 + {"first": 1, "second": 3, "third": 4}[stage]]
-    outs = refs[3 + len(ins) :]
-    result_ref, sent_ref = outs[0], outs[1]
-    inner = pl.program_id(1)
-    y_pair, z_pair, gain = y_ref[0], z_ref[0], gain_ref[0]
+    y_ref, z_ref, gain_ref, *refs = refs
+    *refs, y_pair_ref, z_pair_ref = refs
+    half, inner = pl.program_id(0), pl.program_id(1)
+    chunk = tiles * sublanes
+
+    @pl.when((half == 0) & (inner == 0))
+    def _():
+        prepare(y_ref, z_ref, y_pair_ref, z_pair_ref)
+
+    if stage == "first":
+        state, sent_ref = refs
+    elif stage == "second":
+        crossed, product, forcing, result_ref, sent_ref, slope_ref, turned_ref = refs
+        owners, per = crossed.shape[:2]
+
+        @pl.when(inner == 0)
+        def _():
+            def per_source(s, carry):
+                for k in range(per):
+                    turned_ref[s * per + k] = crossed[s, k, 0].T
+                return carry
+
+            lax.fori_loop(0, owners, per_source, 0)
+
+    else:
+        crossed, product, slope, state, result_ref, sent_ref = refs
+    y_pair, z_pair, gain = y_pair_ref[...], z_pair_ref[...], step_size * gain_ref[0]
 
     def tiled(ref, t, r):
         return ref[0, t, pl.ds(r, grid_y, stride=sublanes), :]
 
-    def arrived(ref, t, r):
-        flat = ref.reshape(grid_y * tiles * sublanes, lanes)
-        return flat[pl.ds(t * sublanes + r, grid_y, stride=tiles * sublanes), :]
+    def across(ref, row):
+        rows = ref.shape[-2]
+        return ref.reshape(grid_y * rows, lanes)[pl.ds(row, grid_y, stride=rows), :]
 
     def per_tile(t, carry):
         for r0 in range(0, sublanes, group):
             each = range(r0, r0 + group)
             if stage == "first":
-                (state,) = ins
                 out = operate([tiled(state, t, r) for r in each], y_pair, z_pair, gain)
-            elif stage == "second":
-                product, crossed, forcing = ins
+                flat = sent_ref.reshape(grid_y * chunk, lanes)
+                for r, value in zip(each, out):
+                    flat[pl.ds(t * sublanes + r, grid_y, stride=chunk), :] = value
+                continue
+            if stage == "second":
                 slopes = [
-                    tiled(product, t, r) + arrived(crossed, t, r) + step_size * tiled(forcing, t, r)
+                    across(product, t * sublanes + r)
+                    + across(turned_ref, inner * chunk + t * sublanes + r)
+                    + step_size * tiled(forcing, t, r)
                     for r in each
                 ]
-                for r, slope in zip(each, slopes):
-                    outs[2][0, t, r] = slope
+                for r, value in zip(each, slopes):
+                    slope_ref[0, t, r] = value
                 out = operate(slopes, y_pair, z_pair, gain)
             else:
-                product, crossed, slope, state = ins
+                arrived = [across(crossed, t * sublanes + r) for r in each]
                 firsts = [
-                    slope[0, t, r] * (1 / 6)
-                    + arrived(crossed, t, r) * 0.125
-                    + tiled(product, t, r) * (1 / 24)
-                    for r in each
+                    slope[0, t, r] * (1 / 6) + value * 0.125 + tiled(product, t, r) * (1 / 24)
+                    for r, value in zip(each, arrived)
                 ]
                 seconds = [
-                    slope[0, t, r] * 0.5 + arrived(crossed, t, r) * (1 / 6) + value
+                    slope[0, t, r] * 0.5 + across(crossed, t * sublanes + r) * (1 / 6) + value
                     for r, value in zip(each, operate(firsts, y_pair, z_pair, gain))
                 ]
                 out = [
@@ -96,7 +125,9 @@
                 result_ref[0, inner * tiles + t, pl.ds(r, grid_y, stride=sublanes), :] = value
         return carry
 
-    lax.fori_loop(0, tiles, per_tile, 0)
+    lax.fori_loop(0, tiles, per_tile, 0, unroll=tiles if stage == "first" else 1)
+    if stage == "first":
+        return
 
     @pl.when(inner == pl.num_programs(1) - 1)
     def _():
@@ -112,7 +143,7 @@
         lax.fori_loop(0, owners, per_owner, 0)
 
 
-def stage_call(stage, harmonic, groups, grid_y, width, y_pair, z_pair, gain, *operands):
+def stage_call(stage, harmonic, groups, grid_y, width, y_operator, z_operator, gain, *operands):
     chunk = tiles * sublanes
     inner = lanes // chunk
     per = width // lanes
@@ -125,40 +156,49 @@
     def tile_spec(which):
         return pl.BlockSpec((1, tiles, rows, lanes), lambda k, i: (which, k * inner + i, 0, 0))
 
-    crossed = pl.BlockSpec((grid_y, chunk, lanes), lambda k, i: (0, k * inner + i, 0))
+    by_rows = pl.BlockSpec((groups, 1, per, chunk, lanes), lambda k, i: (0, k, 0, i, 0))
+    unturned = pl.BlockSpec((groups, per, 1, lanes, lanes), lambda k, i: (0, 0, k, 0, 0))
+    turned = pl.BlockSpec((grid_y, chunk, lanes), lambda k, i: (0, k * inner + i, 0))
     slope = pl.BlockSpec(
         (1, tiles, sublanes, grid_y, lanes), lambda k, i: (0, k * inner + i, 0, 0, 0)
     )
     ins = {
         "first": [tile_spec(harmonic)],
-        "second": [tile_spec(0), crossed, tile_spec(harmonic)],
-        "third": [tile_spec(0), crossed, slope, tile_spec(harmonic)],
+        "second": [unturned, by_rows, tile_spec(harmonic)],
+        "third": [turned, tile_spec(0), slope, tile_spec(harmonic)],
     }[stage]
-    out_specs = [
-        pl.BlockSpec((1, lanes // sublanes, rows, lanes), lambda k, i: (0, k, 0, 0)),
-        pl.BlockSpec((groups, 1, per, lanes, lanes), lambda k, i: (0, k, 0, 0, 0)),
-    ]
-    out_shape = [
-        jax.ShapeDtypeStruct((1, row_tiles, rows, lanes), jnp.float32),
-        jax.ShapeDtypeStruct((groups, per, per, lanes, lanes), jnp.float32),
+    blocks = jax.ShapeDtypeStruct((groups, per, per, lanes, lanes), jnp.float32)
+    if stage == "first":
+        out_specs, out_shape = [by_rows], [blocks]
+    else:
+        out_specs = [
+            pl.BlockSpec((1, lanes // sublanes, rows, lanes), lambda k, i: (0, k, 0, 0)),
+            pl.BlockSpec((groups, 1, per, lanes, lanes), lambda k, i: (0, k, 0, 0, 0)),
+        ]
+        out_shape = [jax.ShapeDtypeStruct((1, row_tiles, rows, lanes), jnp.float32), blocks]
+    scratch = [
+        pltpu.VMEM((2 * grid_y, 2 * grid_y), jnp.bfloat16),
+        pltpu.VMEM((2 * lanes, 2 * lanes), jnp.bfloat16),
     ]
     if stage == "second":
         out_specs.append(slope)
         out_shape.append(
             jax.ShapeDtypeStruct((1, row_tiles, sublanes, grid_y, lanes), jnp.float32)
         )
+        scratch.insert(0, pltpu.VMEM((grid_y, lanes, lanes), jnp.float32))
     passes = 2 if stage == "third" else 1
     return pl.pallas_call(
         functools.partial(body, stage, grid_y),
         grid=(per, inner),
         in_specs=[
-            whole((2 * grid_y, 2 * grid_y)),
-            whole((2 * lanes, 2 * lanes)),
+            whole((grid_y, grid_y)),
+            whole((lanes, lanes)),
             whole((grid_y, lanes)),
             *ins,
         ],
         out_specs=out_specs,
         out_shape=out_shape,
+        scratch_shapes=scratch,
         cost_estimate=pl.CostEstimate(
             flops=passes * 16 * width * grid_y * lanes * (grid_y + lanes),
             bytes_accessed=(len(ins) + len(out_specs)) * width * grid_y * lanes * 4,
@@ -166,7 +206,7 @@
         ),
         compiler_params=pltpu.CompilerParams(vmem_limit_bytes=60 * 1024 * 1024),
         name=f"{stage}_{harmonic}",
-    )(y_pair, z_pair, gain, *operands)
+    )(y_operator, z_operator, gain, *operands)
 
 
 def finish_body(per_step, *refs):
@@ -208,40 +248,35 @@
 
 
 def exchange(sent):
-    received = lax.all_to_all(sent, "col", split_axis=0, concat_axis=0, tiled=True)
-    groups, per = sent.shape[:2]
-    return received.reshape(groups * per, per * lanes, lanes)
+    return lax.all_to_all(sent, "col", split_axis=0, concat_axis=0, tiled=True)
 
 
 def on_device_tiled(covariance, forcing, coefficient, y_operator, z_operator):
     groups = lax.axis_size("col")
     width = covariance.shape[1]
+    per = width // lanes
     grid_y = y_operator.shape[1]
 
     def by_tiles(value):
         cut = value.reshape(2, width // sublanes, sublanes, grid_y, lanes)
         return jnp.swapaxes(cut, 2, 3).reshape(2, width // sublanes, grid_y * sublanes, lanes)
 
-    y_high, y_low = operator_pair(y_operator)
-    z_high, z_low = operator_pair(jnp.swapaxes(z_operator, 1, 2))
-    y_pair = jnp.concatenate(
-        [jnp.concatenate([y_high, y_high], axis=2), jnp.concatenate([y_low, y_low], axis=2)], axis=1
-    )
-    z_pair = jnp.concatenate([jnp.concatenate([z_high, z_low], axis=2)] * 2, axis=1)
-    gain = step_size * coefficient
+    def by_y(blocks):
+        return blocks.reshape(groups * per, per * lanes, lanes)
+
     state, source = by_tiles(covariance), by_tiles(forcing)
 
     def call(stage, harmonic, *operands):
         return stage_call(
-            stage, harmonic, groups, grid_y, width, y_pair, z_pair, gain, *operands
+            stage, harmonic, groups, grid_y, width, y_operator, z_operator, coefficient, *operands
         )
 
-    first = [call("first", h, state) for h in range(2)]
-    crossed = [exchange(sent) for _, sent in first]
-    second = [call("second", h, first[h][0], crossed[h], source) for h in range(2)]
-    crossed = [exchange(sent) for _, sent, _ in second]
-    third = [call("third", h, second[h][0], crossed[h], second[h][2], state) for h in range(2)]
-    crossed = [exchange(sent) for _, sent in third]
+    first = [call("first", h, state)[0] for h in range(2)]
+    crossed = [exchange(sent) for sent in first]
+    second = [call("second", h, crossed[h], first[h], source) for h in range(2)]
+    crossed = [by_y(exchange(sent)) for _, sent, _ in second]
+    third = [call("third", h, crossed[h], second[h][0], second[h][2], state) for h in range(2)]
+    crossed = [by_y(exchange(sent)) for _, sent in third]
     out = None
     for h in range(2):
         out = finish_call(h, third[h][0], crossed[h], out)

time: 1190 us -> 1170 us (0.983)
  transfers between devices with their start and end apart: 6 -> 6, of which waited for: 6 -> 6; matrix products, arithmetic and copies ran while one was open for 0% -> 0% of each run, Pallas kernels for 18% -> 19%
where the time goes in v2:
time: 1170 us
  waiting for transfers between devices  896 us (77%)
  Pallas kernels  248 us (21%)
  starting transfers between devices  25.8 us (2%)
    all_to_all x6, waiting for transfers between devices, exchange(): return lax.all_to_all(sent, 'col', split_axis=0, concat_axis=0, tiled=True)  896 us
    pallas_call x6, Pallas kernels, stage_call(): pl.pallas_call(functools.partial(body, stage, grid_y), grid=(per, inner),...  226 us
    all_to_all x6, starting transfers between devices, exchange(): return lax.all_to_all(sent, 'col', split_axis=0, concat_axis=0, tiled=True)  25.8 us
  transfers between devices with their start and end apart: 6, of which 6 were waited for; matrix products, arithmetic and copies ran while one was open for 0% of the time, Pallas kernels for 19%

profile of v2, /device:TPU:0, one launch (start us, length us, event | category | flops | bytes accessed | tf_op | source)
XLA Modules:
  0.0 1170.0 jit_solution(16695024837947008340)
XLA Ops:
  0.0 17.0 %first_0.1.refs_4_ = f32[32,2,2,128,128]{4,3,2,1,0:T(8,128)} custom-call(f32[2,64,64]{2,1,0:T(8,128)} %refs_0_.11, f32[2,128,128]{2,1,0:T(8,128)} %refs_1_.11, f32[2,64,128]{2,1,0:T(8,128)} %refs_2_.11, f32[2,32,512,128]{3,2,1,0:T(8,128)} %bitcast.14), custom_call_target="tpu_custom_call" | custom-call | flops 6442450944 | bytes 16777216 | tf_op jit(solution)/shard_map/first_0/pallas_call | solution.py:190
  17.0 7.5 all-to-all-start.3
  24.5 17.1 %first_1.1.refs_4_ = f32[32,2,2,128,128]{4,3,2,1,0:T(8,128)} custom-call(f32[2,64,64]{2,1,0:T(8,128)} %refs_0_.11, f32[2,128,128]{2,1,0:T(8,128)} %refs_1_.11, f32[2,64,128]{2,1,0:T(8,128)} %refs_2_.11, f32[2,32,512,128]{3,2,1,0:T(8,128)} %bitcast.15), custom_call_target="tpu_custom_call" | custom-call | flops 6442450944 | bytes 16777216 | tf_op jit(solution)/shard_map/first_1/pallas_call | solution.py:190
  41.6 168.8 %all-to-all-done.3.refs_3_ = f32[32,2,2,128,128]{4,3,2,1,0:T(8,128)} async-done(((f32[32,2,2,128,128]{4,3,2,1,0:T(8,128)}), f32[32,2,2,128,128]{4,3,2,1,0:T(8,128)}, u32[]{:S(2)}, u32[]{:S(2)}) %all-to-all-start.3) | async-done | bytes 8388640 | tf_op jit(solution)/shard_map/all_to_all | solution.py:251
  210.4 3.7 all-to-all-start
  214.1 48.8 %second_0.1 = (f32[1,32,512,128]{3,2,1,0:T(8,128)}, f32[32,2,2,128,128]{4,3,2,1,0:T(8,128)}, f32[1,32,8,64,128]{4,3,2,1,0:T(8,128)}) custom-call(f32[2,64,64]{2,1,0:T(8,128)} %refs_0_.11, f32[2,128,128]{2,1,0:T(8,128)} %refs_1_.11, f32[2,64,128]{2,1,0:T(8,128)} %refs_2_.11, f32[32,2,2,128,128]{4,3,2,1,0:T(8,128)} %all-to-all-done.3.refs_3_, ...), custom_call_target="tpu_custom_call" | custom-call | flops 6442450944 | bytes 50331648 | tf_op jit(solution)/shard_map/second_0/pallas_call | solution.py:190
  262.9 137.3 %all-to-all-done.refs_3_ = f32[32,2,2,128,128]{4,3,2,1,0:T(8,128)} async-done(((f32[32,2,2,128,128]{4,3,2,1,0:T(8,128)}), f32[32,2,2,128,128]{4,3,2,1,0:T(8,128)}, u32[]{:S(2)}, u32[]{:S(2)}) %all-to-all-start) | async-done | bytes 8388640 | tf_op jit(solution)/shard_map/all_to_all | solution.py:251
  400.1 3.7 all-to-all-start.4
  403.8 48.8 %second_1.1 = (f32[1,32,512,128]{3,2,1,0:T(8,128)}, f32[32,2,2,128,128]{4,3,2,1,0:T(8,128)}, f32[1,32,8,64,128]{4,3,2,1,0:T(8,128)}) custom-call(f32[2,64,64]{2,1,0:T(8,128)} %refs_0_.11, f32[2,128,128]{2,1,0:T(8,128)} %refs_1_.11, f32[2,64,128]{2,1,0:T(8,128)} %refs_2_.11, f32[32,2,2,128,128]{4,3,2,1,0:T(8,128)} %all-to-all-done.refs_3_, ...), custom_call_target="tpu_custom_call" | custom-call | flops 6442450944 | bytes 50331648 | tf_op jit(solution)/shard_map/second_1/pallas_call | solution.py:190
  452.6 137.2 %all-to-all-done.4 = f32[32,2,2,128,128]{4,3,2,1,0:T(8,128)} async-done(((f32[32,2,2,128,128]{4,3,2,1,0:T(8,128)}), f32[32,2,2,128,128]{4,3,2,1,0:T(8,128)}, u32[]{:S(2)}, u32[]{:S(2)}) %all-to-all-start.4) | async-done | bytes 8388640 | tf_op jit(solution)/shard_map/all_to_all | solution.py:251
  589.8 3.7 all-to-all-start.1
  593.5 47.4 %third_0.1 = (f32[1,32,512,128]{3,2,1,0:T(8,128)}, f32[32,2,2,128,128]{4,3,2,1,0:T(8,128)}) custom-call(f32[2,64,64]{2,1,0:T(8,128)} %refs_0_.11, f32[2,128,128]{2,1,0:T(8,128)} %refs_1_.11, f32[2,64,128]{2,1,0:T(8,128)} %refs_2_.11, f32[64,256,128]{2,1,0:T(8,128)} %bitcast.12.refs_3_, f32[1,32,512,128]{3,2,1,0:T(8,128)} %get-tuple-element.21.refs_4_, ...), custom_call_target="tpu_custom_call" | custom-call | flops 12884901888 | bytes 50331648 | tf_op jit(solution)/shard_map/third_0/pallas_call | solution.py:190
  640.9 138.6 %all-to-all-done.1 = f32[32,2,2,128,128]{4,3,2,1,0:T(8,128)} async-done(((f32[32,2,2,128,128]{4,3,2,1,0:T(8,128)}), f32[32,2,2,128,128]{4,3,2,1,0:T(8,128)}, u32[]{:S(2)}, u32[]{:S(2)}) %all-to-all-start.1) | async-done | bytes 8388640 | tf_op jit(solution)/shard_map/all_to_all | solution.py:251
  779.6 3.7 all-to-all-start.5
  783.3 47.2 %third_1.1 = (f32[1,32,512,128]{3,2,1,0:T(8,128)}, f32[32,2,2,128,128]{4,3,2,1,0:T(8,128)}) custom-call(f32[2,64,64]{2,1,0:T(8,128)} %refs_0_.11, f32[2,128,128]{2,1,0:T(8,128)} %refs_1_.11, f32[2,64,128]{2,1,0:T(8,128)} %refs_2_.11, f32[64,256,128]{2,1,0:T(8,128)} %bitcast.6.refs_3_, f32[1,32,512,128]{3,2,1,0:T(8,128)} %get-tuple-element.16.refs_4_, ...), custom_call_target="tpu_custom_call" | custom-call | flops 12884901888 | bytes 50331648 | tf_op jit(solution)/shard_map/third_1/pallas_call | solution.py:190
  830.5 138.8 %all-to-all-done.5 = f32[32,2,2,128,128]{4,3,2,1,0:T(8,128)} async-done(((f32[32,2,2,128,128]{4,3,2,1,0:T(8,128)}), f32[32,2,2,128,128]{4,3,2,1,0:T(8,128)}, u32[]{:S(2)}, u32[]{:S(2)}) %all-to-all-start.5) | async-done | bytes 8388640 | tf_op jit(solution)/shard_map/all_to_all | solution.py:251
  969.3 3.7 all-to-all-start.2
  973.0 11.0 finish_0.1.refs_2_
  984.0 175.0 %all-to-all-done.2 = f32[32,2,2,128,128]{4,3,2,1,0:T(8,128)} async-done(((f32[32,2,2,128,128]{4,3,2,1,0:T(8,128)}), f32[32,2,2,128,128]{4,3,2,1,0:T(8,128)}, u32[]{:S(2)}, u32[]{:S(2)}) %all-to-all-start.2) | async-done | bytes 8388640 | tf_op jit(solution)/shard_map/all_to_all | solution.py:251
  1159.0 11.0 finish_1.1
Async XLA Ops:
  17.0 193.4 %all-to-all-start.3 = ((f32[32,2,2,128,128]{4,3,2,1,0:T(8,128)}), f32[32,2,2,128,128]{4,3,2,1,0:T(8,128)}, u32[]{:S(2)}, u32[]{:S(2)}) async-start(f32[32,2,2,128,128]{4,3,2,1,0:T(8,128)} %first_0.1.refs_4_), calls=%async_computation.3 | async-start | bytes 16777216 | tf_op jit(solution)/shard_map/all_to_all | solution.py:251
  210.4 189.7 %all-to-all-start = ((f32[32,2,2,128,128]{4,3,2,1,0:T(8,128)}), f32[32,2,2,128,128]{4,3,2,1,0:T(8,128)}, u32[]{:S(2)}, u32[]{:S(2)}) async-start(f32[32,2,2,128,128]{4,3,2,1,0:T(8,128)} %first_1.1.refs_4_), calls=%async_computation | async-start | bytes 16777216 | tf_op jit(solution)/shard_map/all_to_all | solution.py:251
  400.1 189.7 %all-to-all-start.4 = ((f32[32,2,2,128,128]{4,3,2,1,0:T(8,128)}), f32[32,2,2,128,128]{4,3,2,1,0:T(8,128)}, u32[]{:S(2)}, u32[]{:S(2)}) async-start(f32[32,2,2,128,128]{4,3,2,1,0:T(8,128)} %get-tuple-element.20), calls=%async_computation.4 | async-start | bytes 16777216 | tf_op jit(solution)/shard_map/all_to_all | solution.py:251
  589.8 189.7 %all-to-all-start.1 = ((f32[32,2,2,128,128]{4,3,2,1,0:T(8,128)}), f32[32,2,2,128,128]{4,3,2,1,0:T(8,128)}, u32[]{:S(2)}, u32[]{:S(2)}) async-start(f32[32,2,2,128,128]{4,3,2,1,0:T(8,128)} %get-tuple-element.15), calls=%async_computation.1 | async-start | bytes 16777216 | tf_op jit(solution)/shard_map/all_to_all | solution.py:251
  779.6 189.7 %all-to-all-start.5 = ((f32[32,2,2,128,128]{4,3,2,1,0:T(8,128)}), f32[32,2,2,128,128]{4,3,2,1,0:T(8,128)}, u32[]{:S(2)}, u32[]{:S(2)}) async-start(f32[32,2,2,128,128]{4,3,2,1,0:T(8,128)} %get-tuple-element.24), calls=%async_computation.5 | async-start | bytes 16777216 | tf_op jit(solution)/shard_map/all_to_all | solution.py:251
  969.3 189.7 %all-to-all-start.2 = ((f32[32,2,2,128,128]{4,3,2,1,0:T(8,128)}), f32[32,2,2,128,128]{4,3,2,1,0:T(8,128)}, u32[]{:S(2)}, u32[]{:S(2)}) async-start(f32[32,2,2,128,128]{4,3,2,1,0:T(8,128)} %get-tuple-element.19), calls=%async_computation.2 | async-start | bytes 16777216 | tf_op jit(solution)/shard_map/all_to_all | solution.py:251

commit v3 on v2

--- a/solution.py
+++ b/solution.py
@@ -11,7 +11,7 @@
 lanes = 128
 sublanes = 8
 tiles = 4
-group = 8
+group = sublanes
 
 
 def split(value):
@@ -63,7 +63,7 @@
         prepare(y_ref, z_ref, y_pair_ref, z_pair_ref)
 
     if stage == "first":
-        state, sent_ref = refs
+        state, sent_ref, tile_ref = refs
     elif stage == "second":
         crossed, product, forcing, result_ref, sent_ref, slope_ref, turned_ref = refs
         owners, per = crossed.shape[:2]
@@ -95,7 +95,10 @@
                 out = operate([tiled(state, t, r) for r in each], y_pair, z_pair, gain)
                 flat = sent_ref.reshape(grid_y * chunk, lanes)
                 for r, value in zip(each, out):
-                    flat[pl.ds(t * sublanes + r, grid_y, stride=chunk), :] = value
+                    tile_ref[t, pl.ds(r, grid_y, stride=sublanes), :] = value
+                for y in range(grid_y):
+                    start = pl.multiple_of(y * chunk + t * sublanes, sublanes)
+                    flat[pl.ds(start, sublanes), :] = tile_ref[t, pl.ds(y * sublanes, sublanes), :]
                 continue
             if stage == "second":
                 slopes = [
@@ -186,6 +189,8 @@
             jax.ShapeDtypeStruct((1, row_tiles, sublanes, grid_y, lanes), jnp.float32)
         )
         scratch.insert(0, pltpu.VMEM((grid_y, lanes, lanes), jnp.float32))
+    if stage == "first":
+        scratch.insert(0, pltpu.VMEM((tiles, rows, lanes), jnp.float32))
     passes = 2 if stage == "third" else 1
     return pl.pallas_call(
         functools.partial(body, stage, grid_y),
@@ -209,20 +214,20 @@
     )(y_operator, z_operator, gain, *operands)
 
 
-def finish_body(per_step, *refs):
+def finish_body(*refs):
     product_ref, crossed_ref, out_ref = refs[0], refs[1], refs[-1]
-    for j in range(per_step):
-        half = product_ref[0, :, j * sublanes : (j + 1) * sublanes, :]
-        out_ref[0, :, j * lanes : (j + 1) * lanes] = half.reshape(-1, lanes) + crossed_ref[j]
+    for y in range(crossed_ref.shape[0]):
+        part = product_ref[0, :, y * sublanes : (y + 1) * sublanes, :]
+        out_ref[0, :, y * lanes : (y + 1) * lanes] = part.reshape(-1, lanes) + crossed_ref[y]
 
 
 def finish_call(harmonic, product, crossed, out):
     grid_y, width, _ = crossed.shape
-    per_step = 8 if grid_y % 8 == 0 else 1
-    row_tiles = width // sublanes
+    row_tiles = lanes // sublanes // 2
+    chunk = row_tiles * sublanes
     in_specs = [
-        pl.BlockSpec((1, row_tiles, per_step * sublanes, lanes), lambda i: (0, 0, i, 0)),
-        pl.BlockSpec((per_step, width, lanes), lambda i: (i, 0, 0)),
+        pl.BlockSpec((1, row_tiles, grid_y * sublanes, lanes), lambda i: (0, i, 0, 0)),
+        pl.BlockSpec((grid_y, chunk, lanes), lambda i: (0, i, 0)),
     ]
     operands = [product, crossed]
     aliases = {}
@@ -231,10 +236,10 @@
         operands.append(out)
         aliases = {2: 0}
     return pl.pallas_call(
-        functools.partial(finish_body, per_step),
-        grid=(grid_y // per_step,),
+        finish_body,
+        grid=(width // chunk,),
         in_specs=in_specs,
-        out_specs=pl.BlockSpec((1, width, per_step * lanes), lambda i: (harmonic, 0, i)),
+        out_specs=pl.BlockSpec((1, chunk, grid_y * lanes), lambda i: (harmonic, i, 0)),
         out_shape=jax.ShapeDtypeStruct((2, width, grid_y * lanes), jnp.float32),
         input_output_aliases=aliases,
         cost_estimate=pl.CostEstimate(
@@ -242,7 +247,7 @@
             bytes_accessed=3 * width * grid_y * lanes * 4,
             transcendentals=0,
         ),
-        compiler_params=pltpu.CompilerParams(vmem_limit_bytes=48 * 1024 * 1024),
+        compiler_params=pltpu.CompilerParams(vmem_limit_bytes=60 * 1024 * 1024),
         name=f"finish_{harmonic}",
     )(*operands)
 

time: 1170 us -> 1170 us (level)
  no operation moved by 1% of the time
where the time goes in v3:
time: 1170 us
  waiting for transfers between devices  900 us (77%)
  Pallas kernels  240 us (21%)
  starting transfers between devices  25.8 us (2%)
    all_to_all x6, waiting for transfers between devices, exchange(): return lax.all_to_all(sent, 'col', split_axis=0, concat_axis=0, tiled=True)  900 us
    pallas_call x6, Pallas kernels, stage_call(): pl.pallas_call(functools.partial(body, stage, grid_y), grid=(per, inner),...  222 us
    all_to_all x6, starting transfers between devices, exchange(): return lax.all_to_all(sent, 'col', split_axis=0, concat_axis=0, tiled=True)  25.8 us
  transfers between devices with their start and end apart: 6, of which 6 were waited for; matrix products, arithmetic and copies ran while one was open for 0% of the time, Pallas kernels for 19%

profile of v3, /device:TPU:0, one launch (start us, length us, event | category | flops | bytes accessed | tf_op | source)
XLA Modules:
  0.0 1165.9 jit_solution(2398948659215897236)
XLA Ops:
  0.0 15.0 %first_0.1.refs_4_ = f32[32,2,2,128,128]{4,3,2,1,0:T(8,128)} custom-call(f32[2,64,64]{2,1,0:T(8,128)} %refs_0_.11, f32[2,128,128]{2,1,0:T(8,128)} %refs_1_.11, f32[2,64,128]{2,1,0:T(8,128)} %refs_2_.11, f32[2,32,512,128]{3,2,1,0:T(8,128)} %bitcast.14), custom_call_target="tpu_custom_call" | custom-call | flops 6442450944 | bytes 16777216 | tf_op jit(solution)/shard_map/first_0/pallas_call | solution.py:195
  15.0 7.5 all-to-all-start.3
  22.4 15.0 %first_1.1.refs_4_ = f32[32,2,2,128,128]{4,3,2,1,0:T(8,128)} custom-call(f32[2,64,64]{2,1,0:T(8,128)} %refs_0_.11, f32[2,128,128]{2,1,0:T(8,128)} %refs_1_.11, f32[2,64,128]{2,1,0:T(8,128)} %refs_2_.11, f32[2,32,512,128]{3,2,1,0:T(8,128)} %bitcast.15), custom_call_target="tpu_custom_call" | custom-call | flops 6442450944 | bytes 16777216 | tf_op jit(solution)/shard_map/first_1/pallas_call | solution.py:195
  37.4 170.9 %all-to-all-done.3.refs_3_ = f32[32,2,2,128,128]{4,3,2,1,0:T(8,128)} async-done(((f32[32,2,2,128,128]{4,3,2,1,0:T(8,128)}), f32[32,2,2,128,128]{4,3,2,1,0:T(8,128)}, u32[]{:S(2)}, u32[]{:S(2)}) %all-to-all-start.3) | async-done | bytes 8388640 | tf_op jit(solution)/shard_map/all_to_all | solution.py:256
  208.3 3.7 all-to-all-start
  212.0 48.8 %second_0.1 = (f32[1,32,512,128]{3,2,1,0:T(8,128)}, f32[32,2,2,128,128]{4,3,2,1,0:T(8,128)}, f32[1,32,8,64,128]{4,3,2,1,0:T(8,128)}) custom-call(f32[2,64,64]{2,1,0:T(8,128)} %refs_0_.11, f32[2,128,128]{2,1,0:T(8,128)} %refs_1_.11, f32[2,64,128]{2,1,0:T(8,128)} %refs_2_.11, f32[32,2,2,128,128]{4,3,2,1,0:T(8,128)} %all-to-all-done.3.refs_3_, ...), custom_call_target="tpu_custom_call" | custom-call | flops 6442450944 | bytes 50331648 | tf_op jit(solution)/shard_map/second_0/pallas_call | solution.py:195
  260.8 137.3 %all-to-all-done.refs_3_ = f32[32,2,2,128,128]{4,3,2,1,0:T(8,128)} async-done(((f32[32,2,2,128,128]{4,3,2,1,0:T(8,128)}), f32[32,2,2,128,128]{4,3,2,1,0:T(8,128)}, u32[]{:S(2)}, u32[]{:S(2)}) %all-to-all-start) | async-done | bytes 8388640 | tf_op jit(solution)/shard_map/all_to_all | solution.py:256
  398.1 3.7 all-to-all-start.4
  401.7 48.8 %second_1.1 = (f32[1,32,512,128]{3,2,1,0:T(8,128)}, f32[32,2,2,128,128]{4,3,2,1,0:T(8,128)}, f32[1,32,8,64,128]{4,3,2,1,0:T(8,128)}) custom-call(f32[2,64,64]{2,1,0:T(8,128)} %refs_0_.11, f32[2,128,128]{2,1,0:T(8,128)} %refs_1_.11, f32[2,64,128]{2,1,0:T(8,128)} %refs_2_.11, f32[32,2,2,128,128]{4,3,2,1,0:T(8,128)} %all-to-all-done.refs_3_, ...), custom_call_target="tpu_custom_call" | custom-call | flops 6442450944 | bytes 50331648 | tf_op jit(solution)/shard_map/second_1/pallas_call | solution.py:195
  450.5 137.2 %all-to-all-done.4 = f32[32,2,2,128,128]{4,3,2,1,0:T(8,128)} async-done(((f32[32,2,2,128,128]{4,3,2,1,0:T(8,128)}), f32[32,2,2,128,128]{4,3,2,1,0:T(8,128)}, u32[]{:S(2)}, u32[]{:S(2)}) %all-to-all-start.4) | async-done | bytes 8388640 | tf_op jit(solution)/shard_map/all_to_all | solution.py:256
  587.8 3.7 all-to-all-start.1
  591.5 47.4 %third_0.1 = (f32[1,32,512,128]{3,2,1,0:T(8,128)}, f32[32,2,2,128,128]{4,3,2,1,0:T(8,128)}) custom-call(f32[2,64,64]{2,1,0:T(8,128)} %refs_0_.11, f32[2,128,128]{2,1,0:T(8,128)} %refs_1_.11, f32[2,64,128]{2,1,0:T(8,128)} %refs_2_.11, f32[64,256,128]{2,1,0:T(8,128)} %bitcast.12.refs_3_, f32[1,32,512,128]{3,2,1,0:T(8,128)} %get-tuple-element.21.refs_4_, ...), custom_call_target="tpu_custom_call" | custom-call | flops 12884901888 | bytes 50331648 | tf_op jit(solution)/shard_map/third_0/pallas_call | solution.py:195
  638.9 138.6 %all-to-all-done.1 = f32[32,2,2,128,128]{4,3,2,1,0:T(8,128)} async-done(((f32[32,2,2,128,128]{4,3,2,1,0:T(8,128)}), f32[32,2,2,128,128]{4,3,2,1,0:T(8,128)}, u32[]{:S(2)}, u32[]{:S(2)}) %all-to-all-start.1) | async-done | bytes 8388640 | tf_op jit(solution)/shard_map/all_to_all | solution.py:256
  777.5 3.7 all-to-all-start.5
  781.2 47.2 %third_1.1 = (f32[1,32,512,128]{3,2,1,0:T(8,128)}, f32[32,2,2,128,128]{4,3,2,1,0:T(8,128)}) custom-call(f32[2,64,64]{2,1,0:T(8,128)} %refs_0_.11, f32[2,128,128]{2,1,0:T(8,128)} %refs_1_.11, f32[2,64,128]{2,1,0:T(8,128)} %refs_2_.11, f32[64,256,128]{2,1,0:T(8,128)} %bitcast.6.refs_3_, f32[1,32,512,128]{3,2,1,0:T(8,128)} %get-tuple-element.16.refs_4_, ...), custom_call_target="tpu_custom_call" | custom-call | flops 12884901888 | bytes 50331648 | tf_op jit(solution)/shard_map/third_1/pallas_call | solution.py:195
  828.4 138.8 %all-to-all-done.5 = f32[32,2,2,128,128]{4,3,2,1,0:T(8,128)} async-done(((f32[32,2,2,128,128]{4,3,2,1,0:T(8,128)}), f32[32,2,2,128,128]{4,3,2,1,0:T(8,128)}, u32[]{:S(2)}, u32[]{:S(2)}) %all-to-all-start.5) | async-done | bytes 8388640 | tf_op jit(solution)/shard_map/all_to_all | solution.py:256
  967.2 3.7 all-to-all-start.2
  970.9 9.0 finish_0.1.refs_2_
  979.9 177.1 %all-to-all-done.2 = f32[32,2,2,128,128]{4,3,2,1,0:T(8,128)} async-done(((f32[32,2,2,128,128]{4,3,2,1,0:T(8,128)}), f32[32,2,2,128,128]{4,3,2,1,0:T(8,128)}, u32[]{:S(2)}, u32[]{:S(2)}) %all-to-all-start.2) | async-done | bytes 8388640 | tf_op jit(solution)/shard_map/all_to_all | solution.py:256
  1156.9 8.9 finish_1.1
Async XLA Ops:
  15.0 193.4 %all-to-all-start.3 = ((f32[32,2,2,128,128]{4,3,2,1,0:T(8,128)}), f32[32,2,2,128,128]{4,3,2,1,0:T(8,128)}, u32[]{:S(2)}, u32[]{:S(2)}) async-start(f32[32,2,2,128,128]{4,3,2,1,0:T(8,128)} %first_0.1.refs_4_), calls=%async_computation.3 | async-start | bytes 16777216 | tf_op jit(solution)/shard_map/all_to_all | solution.py:256
  208.3 189.7 %all-to-all-start = ((f32[32,2,2,128,128]{4,3,2,1,0:T(8,128)}), f32[32,2,2,128,128]{4,3,2,1,0:T(8,128)}, u32[]{:S(2)}, u32[]{:S(2)}) async-start(f32[32,2,2,128,128]{4,3,2,1,0:T(8,128)} %first_1.1.refs_4_), calls=%async_computation | async-start | bytes 16777216 | tf_op jit(solution)/shard_map/all_to_all | solution.py:256
  398.1 189.7 %all-to-all-start.4 = ((f32[32,2,2,128,128]{4,3,2,1,0:T(8,128)}), f32[32,2,2,128,128]{4,3,2,1,0:T(8,128)}, u32[]{:S(2)}, u32[]{:S(2)}) async-start(f32[32,2,2,128,128]{4,3,2,1,0:T(8,128)} %get-tuple-element.20), calls=%async_computation.4 | async-start | bytes 16777216 | tf_op jit(solution)/shard_map/all_to_all | solution.py:256
  587.8 189.7 %all-to-all-start.1 = ((f32[32,2,2,128,128]{4,3,2,1,0:T(8,128)}), f32[32,2,2,128,128]{4,3,2,1,0:T(8,128)}, u32[]{:S(2)}, u32[]{:S(2)}) async-start(f32[32,2,2,128,128]{4,3,2,1,0:T(8,128)} %get-tuple-element.15), calls=%async_computation.1 | async-start | bytes 16777216 | tf_op jit(solution)/shard_map/all_to_all | solution.py:256
  777.5 189.7 %all-to-all-start.5 = ((f32[32,2,2,128,128]{4,3,2,1,0:T(8,128)}), f32[32,2,2,128,128]{4,3,2,1,0:T(8,128)}, u32[]{:S(2)}, u32[]{:S(2)}) async-start(f32[32,2,2,128,128]{4,3,2,1,0:T(8,128)} %get-tuple-element.24), calls=%async_computation.5 | async-start | bytes 16777216 | tf_op jit(solution)/shard_map/all_to_all | solution.py:256
  967.2 189.7 %all-to-all-start.2 = ((f32[32,2,2,128,128]{4,3,2,1,0:T(8,128)}), f32[32,2,2,128,128]{4,3,2,1,0:T(8,128)}, u32[]{:S(2)}, u32[]{:S(2)}) async-start(f32[32,2,2,128,128]{4,3,2,1,0:T(8,128)} %get-tuple-element.19), calls=%async_computation.2 | async-start | bytes 16777216 | tf_op jit(solution)/shard_map/all_to_all | solution.py:256

commit v4 on v3

--- a/solution.py
+++ b/solution.py
@@ -10,7 +10,7 @@
 step_size = 0.2
 lanes = 128
 sublanes = 8
-tiles = 4
+tiles = 8
 group = sublanes
 
 
@@ -63,7 +63,7 @@
         prepare(y_ref, z_ref, y_pair_ref, z_pair_ref)
 
     if stage == "first":
-        state, sent_ref, tile_ref = refs
+        state, sent_ref = refs
     elif stage == "second":
         crossed, product, forcing, result_ref, sent_ref, slope_ref, turned_ref = refs
         owners, per = crossed.shape[:2]
@@ -94,11 +94,12 @@
             if stage == "first":
                 out = operate([tiled(state, t, r) for r in each], y_pair, z_pair, gain)
                 flat = sent_ref.reshape(grid_y * chunk, lanes)
-                for r, value in zip(each, out):
-                    tile_ref[t, pl.ds(r, grid_y, stride=sublanes), :] = value
-                for y in range(grid_y):
-                    start = pl.multiple_of(y * chunk + t * sublanes, sublanes)
-                    flat[pl.ds(start, sublanes), :] = tile_ref[t, pl.ds(y * sublanes, sublanes), :]
+                for j in range(0, grid_y, sublanes):
+                    cube = jnp.stack([value[j : j + sublanes] for value in out])
+                    cube = jnp.swapaxes(cube, 0, 1)
+                    for y in range(sublanes):
+                        start = pl.multiple_of((j + y) * chunk + t * sublanes, sublanes)
+                        flat[pl.ds(start, sublanes), :] = cube[y]
                 continue
             if stage == "second":
                 slopes = [
@@ -189,8 +190,6 @@
             jax.ShapeDtypeStruct((1, row_tiles, sublanes, grid_y, lanes), jnp.float32)
         )
         scratch.insert(0, pltpu.VMEM((grid_y, lanes, lanes), jnp.float32))
-    if stage == "first":
-        scratch.insert(0, pltpu.VMEM((tiles, rows, lanes), jnp.float32))
     passes = 2 if stage == "third" else 1
     return pl.pallas_call(
         functools.partial(body, stage, grid_y),

time: 1170 us -> 1170 us (level)
  no operation moved by 1% of the time
where the time goes in v4:
time: 1170 us
  waiting for transfers between devices  899 us (77%)
  Pallas kernels  240 us (21%)
  starting transfers between devices  25.8 us (2%)
    all_to_all x6, waiting for transfers between devices, exchange(): return lax.all_to_all(sent, 'col', split_axis=0, concat_axis=0, tiled=True)  899 us
    pallas_call x6, Pallas kernels, stage_call(): pl.pallas_call(functools.partial(body, stage, grid_y), grid=(per, inner),...  222 us
    all_to_all x6, starting transfers between devices, exchange(): return lax.all_to_all(sent, 'col', split_axis=0, concat_axis=0, tiled=True)  25.8 us
  transfers between devices with their start and end apart: 6, of which 6 were waited for; matrix products, arithmetic and copies ran while one was open for 0% of the time, Pallas kernels for 19%

profile of v4, /device:TPU:0, one launch (start us, length us, event | category | flops | bytes accessed | tf_op | source)
XLA Modules:
  0.0 1165.1 jit_solution(7431065067994235762)
XLA Ops:
  0.0 14.2 %first_0.1.refs_4_ = f32[32,2,2,128,128]{4,3,2,1,0:T(8,128)} custom-call(f32[2,64,64]{2,1,0:T(8,128)} %refs_0_.11, f32[2,128,128]{2,1,0:T(8,128)} %refs_1_.11, f32[2,64,128]{2,1,0:T(8,128)} %refs_2_.11, f32[2,32,512,128]{3,2,1,0:T(8,128)} %bitcast.14), custom_call_target="tpu_custom_call" | custom-call | flops 6442450944 | bytes 16777216 | tf_op jit(solution)/shard_map/first_0/pallas_call | solution.py:194
  14.2 7.5 all-to-all-start.3
  21.7 14.2 %first_1.1.refs_4_ = f32[32,2,2,128,128]{4,3,2,1,0:T(8,128)} custom-call(f32[2,64,64]{2,1,0:T(8,128)} %refs_0_.11, f32[2,128,128]{2,1,0:T(8,128)} %refs_1_.11, f32[2,64,128]{2,1,0:T(8,128)} %refs_2_.11, f32[2,32,512,128]{3,2,1,0:T(8,128)} %bitcast.15), custom_call_target="tpu_custom_call" | custom-call | flops 6442450944 | bytes 16777216 | tf_op jit(solution)/shard_map/first_1/pallas_call | solution.py:194
  35.9 171.7 %all-to-all-done.3.refs_3_ = f32[32,2,2,128,128]{4,3,2,1,0:T(8,128)} async-done(((f32[32,2,2,128,128]{4,3,2,1,0:T(8,128)}), f32[32,2,2,128,128]{4,3,2,1,0:T(8,128)}, u32[]{:S(2)}, u32[]{:S(2)}) %all-to-all-start.3) | async-done | bytes 8388640 | tf_op jit(solution)/shard_map/all_to_all | solution.py:255
  207.6 3.7 all-to-all-start
  211.2 49.3 %second_0.1 = (f32[1,32,512,128]{3,2,1,0:T(8,128)}, f32[32,2,2,128,128]{4,3,2,1,0:T(8,128)}, f32[1,32,8,64,128]{4,3,2,1,0:T(8,128)}) custom-call(f32[2,64,64]{2,1,0:T(8,128)} %refs_0_.11, f32[2,128,128]{2,1,0:T(8,128)} %refs_1_.11, f32[2,64,128]{2,1,0:T(8,128)} %refs_2_.11, f32[32,2,2,128,128]{4,3,2,1,0:T(8,128)} %all-to-all-done.3.refs_3_, ...), custom_call_target="tpu_custom_call" | custom-call | flops 6442450944 | bytes 50331648 | tf_op jit(solution)/shard_map/second_0/pallas_call | solution.py:194
  260.5 136.8 %all-to-all-done.refs_3_ = f32[32,2,2,128,128]{4,3,2,1,0:T(8,128)} async-done(((f32[32,2,2,128,128]{4,3,2,1,0:T(8,128)}), f32[32,2,2,128,128]{4,3,2,1,0:T(8,128)}, u32[]{:S(2)}, u32[]{:S(2)}) %all-to-all-start) | async-done | bytes 8388640 | tf_op jit(solution)/shard_map/all_to_all | solution.py:255
  397.3 3.7 all-to-all-start.4
  401.0 49.3 %second_1.1 = (f32[1,32,512,128]{3,2,1,0:T(8,128)}, f32[32,2,2,128,128]{4,3,2,1,0:T(8,128)}, f32[1,32,8,64,128]{4,3,2,1,0:T(8,128)}) custom-call(f32[2,64,64]{2,1,0:T(8,128)} %refs_0_.11, f32[2,128,128]{2,1,0:T(8,128)} %refs_1_.11, f32[2,64,128]{2,1,0:T(8,128)} %refs_2_.11, f32[32,2,2,128,128]{4,3,2,1,0:T(8,128)} %all-to-all-done.refs_3_, ...), custom_call_target="tpu_custom_call" | custom-call | flops 6442450944 | bytes 50331648 | tf_op jit(solution)/shard_map/second_1/pallas_call | solution.py:194
  450.2 136.8 %all-to-all-done.4 = f32[32,2,2,128,128]{4,3,2,1,0:T(8,128)} async-done(((f32[32,2,2,128,128]{4,3,2,1,0:T(8,128)}), f32[32,2,2,128,128]{4,3,2,1,0:T(8,128)}, u32[]{:S(2)}, u32[]{:S(2)}) %all-to-all-start.4) | async-done | bytes 8388640 | tf_op jit(solution)/shard_map/all_to_all | solution.py:255
  587.0 3.7 all-to-all-start.1
  590.7 47.7 %third_0.1 = (f32[1,32,512,128]{3,2,1,0:T(8,128)}, f32[32,2,2,128,128]{4,3,2,1,0:T(8,128)}) custom-call(f32[2,64,64]{2,1,0:T(8,128)} %refs_0_.11, f32[2,128,128]{2,1,0:T(8,128)} %refs_1_.11, f32[2,64,128]{2,1,0:T(8,128)} %refs_2_.11, f32[64,256,128]{2,1,0:T(8,128)} %bitcast.12.refs_3_, f32[1,32,512,128]{3,2,1,0:T(8,128)} %get-tuple-element.21.refs_4_, ...), custom_call_target="tpu_custom_call" | custom-call | flops 12884901888 | bytes 50331648 | tf_op jit(solution)/shard_map/third_0/pallas_call | solution.py:194
  638.4 138.4 %all-to-all-done.1 = f32[32,2,2,128,128]{4,3,2,1,0:T(8,128)} async-done(((f32[32,2,2,128,128]{4,3,2,1,0:T(8,128)}), f32[32,2,2,128,128]{4,3,2,1,0:T(8,128)}, u32[]{:S(2)}, u32[]{:S(2)}) %all-to-all-start.1) | async-done | bytes 8388640 | tf_op jit(solution)/shard_map/all_to_all | solution.py:255
  776.7 3.7 all-to-all-start.5
  780.4 47.5 %third_1.1 = (f32[1,32,512,128]{3,2,1,0:T(8,128)}, f32[32,2,2,128,128]{4,3,2,1,0:T(8,128)}) custom-call(f32[2,64,64]{2,1,0:T(8,128)} %refs_0_.11, f32[2,128,128]{2,1,0:T(8,128)} %refs_1_.11, f32[2,64,128]{2,1,0:T(8,128)} %refs_2_.11, f32[64,256,128]{2,1,0:T(8,128)} %bitcast.6.refs_3_, f32[1,32,512,128]{3,2,1,0:T(8,128)} %get-tuple-element.16.refs_4_, ...), custom_call_target="tpu_custom_call" | custom-call | flops 12884901888 | bytes 50331648 | tf_op jit(solution)/shard_map/third_1/pallas_call | solution.py:194
  827.9 138.6 %all-to-all-done.5 = f32[32,2,2,128,128]{4,3,2,1,0:T(8,128)} async-done(((f32[32,2,2,128,128]{4,3,2,1,0:T(8,128)}), f32[32,2,2,128,128]{4,3,2,1,0:T(8,128)}, u32[]{:S(2)}, u32[]{:S(2)}) %all-to-all-start.5) | async-done | bytes 8388640 | tf_op jit(solution)/shard_map/all_to_all | solution.py:255
  966.4 3.7 all-to-all-start.2
  970.1 9.0 finish_0.1.refs_2_
  979.1 177.1 %all-to-all-done.2 = f32[32,2,2,128,128]{4,3,2,1,0:T(8,128)} async-done(((f32[32,2,2,128,128]{4,3,2,1,0:T(8,128)}), f32[32,2,2,128,128]{4,3,2,1,0:T(8,128)}, u32[]{:S(2)}, u32[]{:S(2)}) %all-to-all-start.2) | async-done | bytes 8388640 | tf_op jit(solution)/shard_map/all_to_all | solution.py:255
  1156.2 8.9 finish_1.1
Async XLA Ops:
  14.2 193.4 %all-to-all-start.3 = ((f32[32,2,2,128,128]{4,3,2,1,0:T(8,128)}), f32[32,2,2,128,128]{4,3,2,1,0:T(8,128)}, u32[]{:S(2)}, u32[]{:S(2)}) async-start(f32[32,2,2,128,128]{4,3,2,1,0:T(8,128)} %first_0.1.refs_4_), calls=%async_computation.3 | async-start | bytes 16777216 | tf_op jit(solution)/shard_map/all_to_all | solution.py:255
  207.6 189.7 %all-to-all-start = ((f32[32,2,2,128,128]{4,3,2,1,0:T(8,128)}), f32[32,2,2,128,128]{4,3,2,1,0:T(8,128)}, u32[]{:S(2)}, u32[]{:S(2)}) async-start(f32[32,2,2,128,128]{4,3,2,1,0:T(8,128)} %first_1.1.refs_4_), calls=%async_computation | async-start | bytes 16777216 | tf_op jit(solution)/shard_map/all_to_all | solution.py:255
  397.3 189.7 %all-to-all-start.4 = ((f32[32,2,2,128,128]{4,3,2,1,0:T(8,128)}), f32[32,2,2,128,128]{4,3,2,1,0:T(8,128)}, u32[]{:S(2)}, u32[]{:S(2)}) async-start(f32[32,2,2,128,128]{4,3,2,1,0:T(8,128)} %get-tuple-element.20), calls=%async_computation.4 | async-start | bytes 16777216 | tf_op jit(solution)/shard_map/all_to_all | solution.py:255
  587.0 189.7 %all-to-all-start.1 = ((f32[32,2,2,128,128]{4,3,2,1,0:T(8,128)}), f32[32,2,2,128,128]{4,3,2,1,0:T(8,128)}, u32[]{:S(2)}, u32[]{:S(2)}) async-start(f32[32,2,2,128,128]{4,3,2,1,0:T(8,128)} %get-tuple-element.15), calls=%async_computation.1 | async-start | bytes 16777216 | tf_op jit(solution)/shard_map/all_to_all | solution.py:255
  776.7 189.7 %all-to-all-start.5 = ((f32[32,2,2,128,128]{4,3,2,1,0:T(8,128)}), f32[32,2,2,128,128]{4,3,2,1,0:T(8,128)}, u32[]{:S(2)}, u32[]{:S(2)}) async-start(f32[32,2,2,128,128]{4,3,2,1,0:T(8,128)} %get-tuple-element.24), calls=%async_computation.5 | async-start | bytes 16777216 | tf_op jit(solution)/shard_map/all_to_all | solution.py:255
  966.4 189.7 %all-to-all-start.2 = ((f32[32,2,2,128,128]{4,3,2,1,0:T(8,128)}), f32[32,2,2,128,128]{4,3,2,1,0:T(8,128)}, u32[]{:S(2)}, u32[]{:S(2)}) async-start(f32[32,2,2,128,128]{4,3,2,1,0:T(8,128)} %get-tuple-element.19), calls=%async_computation.2 | async-start | bytes 16777216 | tf_op jit(solution)/shard_map/all_to_all | solution.py:255
